TPU v7x, 128 devices: a whole 4x4x4 slice. The times are simulated.
128 devices in a mesh: tile: 8 (over x_hi, z), src: 16 (over y, x_lo, core).
Axes of the slice: x: 4 (x_hi: 2, x_lo: 2; x = x_hi * 2 + x_lo), y: 4, z: 4, core: 2. Of those that a mesh axis runs over, the one named last changes fastest.
Arguments:
- permittivity: float32 [128, 16, 320], P(('tile', 'src')), may hold values from 1 to 2
- e_start: float32 [16, 3, 128, 16, 320], P('src', None, 'tile'), may hold values from -6 to 6
- h_start: float32 [16, 3, 128, 16, 320], P('src', None, 'tile'), may hold values from -6 to 6
- e_cotangent: float32 [16, 3, 128, 16, 320], P('src', None, 'tile'), may hold values from -6 to 6
- h_cotangent: float32 [16, 3, 128, 16, 320], P('src', None, 'tile'), may hold values from -6 to 6
Outputs:
- e_final: float32 [16, 3, 128, 16, 320], P('src', None, 'tile')
- gradient: float32 [128, 16, 320], P(('tile', 'src'))
All inputs are finite; a program needn't handle non-finite values.
Results may differ from a plain program's by a relative error of at most 0.00002.
Values sent between devices are 32-bit elements; how exact they have to be, the bound alone decides.
No kernel may reach another device: no remote copies, remote signals or barrier semaphores. Data moves between devices by JAX's collectives and lax.ppermute only.
A program may use at most 64 MiB of HBM per device.

v0:
```python
import jax
import jax.numpy as jnp
from jax import lax
from jax.sharding import PartitionSpec as P

STEPS = 6
courant = 0.57


def passed_along(array, axis, by):
    length = lax.axis_size(axis)
    pairs = [(i, i + by) for i in range(length) if 0 <= i + by < length]
    return lax.ppermute(array, axis, pairs)


def ahead_local(field, axis):
    size = field.shape[axis]
    upper = lax.slice_in_dim(field, 1, size, axis=axis)
    zeros = jnp.zeros_like(lax.slice_in_dim(field, 0, 1, axis=axis))
    return jnp.concatenate([upper, zeros], axis) - field


def behind_local(field, axis):
    size = field.shape[axis]
    lower = lax.slice_in_dim(field, 0, size - 1, axis=axis)
    zeros = jnp.zeros_like(lax.slice_in_dim(field, 0, 1, axis=axis))
    return field - jnp.concatenate([zeros, lower], axis)


def curl_ahead(field):
    border = passed_along(field[1:3, 0:1], "tile", -1)
    ahead_one = jnp.concatenate([field[1, 1:], border[0]], 0) - field[1]
    ahead_two = jnp.concatenate([field[2, 1:], border[1]], 0) - field[2]
    return jnp.stack(
        [
            ahead_local(field[2], 1) - ahead_local(field[1], 2),
            ahead_local(field[0], 2) - ahead_two,
            ahead_one - ahead_local(field[0], 1),
        ]
    )


def curl_behind(field):
    border = passed_along(field[1:3, -1:], "tile", 1)
    behind_one = field[1] - jnp.concatenate([border[0], field[1, :-1]], 0)
    behind_two = field[2] - jnp.concatenate([border[1], field[2, :-1]], 0)
    return jnp.stack(
        [
            behind_local(field[2], 1) - behind_local(field[1], 2),
            behind_local(field[0], 2) - behind_two,
            behind_one - behind_local(field[0], 1),
        ]
    )


def add_term(term, shard_total, local_total):
    shard_total = shard_total + lax.psum_scatter(term, "src", scatter_dimension=0, tiled=True)
    return (shard_total, local_total)


def on_device(permittivity, e_start, h_start, e_cotangent, h_cotangent):
    window = lax.all_gather(permittivity, "src", axis=0, tiled=True)
    inverse = 1.0 / window
    efield = e_start[0]
    hfield = h_start[0]
    stored = []
    for turn in range(STEPS):
        hfield = hfield - courant * curl_ahead(efield)
        curled = curl_behind(hfield)
        efield = efield + courant * inverse * curled
        stored.append(curled)
    adj_efield = e_cotangent[0]
    adj_hfield = h_cotangent[0]
    shard_total = jnp.zeros(permittivity.shape, jnp.float32)
    local_total = jnp.zeros(window.shape, jnp.float32)
    for turn in range(STEPS - 1, -1, -1):
        curled = stored[turn]
        term = courant * jnp.sum(adj_efield * curled, axis=0)
        shard_total, local_total = add_term(term, shard_total, local_total)
        adj_hfield = adj_hfield + courant * curl_ahead(inverse * adj_efield)
        adj_efield = adj_efield - courant * curl_behind(adj_hfield)
    gradient = -shard_total / (permittivity * permittivity)
    return (efield[None], gradient)


def solution(mesh):
    in_specs = (
        P(("tile", "src"), None, None),
        P("src", None, "tile", None, None),
        P("src", None, "tile", None, None),
        P("src", None, "tile", None, None),
        P("src", None, "tile", None, None),
    )
    out_specs = (P("src", None, "tile", None, None), P(("tile", "src"), None, None))
    return jax.shard_map(
        on_device, mesh=mesh, in_specs=in_specs, out_specs=out_specs, check_vma=False
    )
```

profile of v0, /device:TPU:0, one launch (start us, length us, event | category | flops | bytes accessed | tf_op | source)
XLA Modules:
  0.0 292.2 jit_solution(3197136223210983773)
XLA Ops:
  10.8 21.7 %all_gather.3 = f32[16,16,320]{2,1,0:T(8,128)S(1)} all-gather(f32[1,16,320]{2,1,0:T(8,128)S(1)} %copy-done.17), channel_id=1, replica_groups=mesh['tile'=8,'src'=16] {'src'}, dimensions={0}, use_global_device_ids=true | all-gather | bytes 348160 | tf_op jit(solution)/shard_map/all_gather | solution.py:62
  34.6 4.5 %collective-permute-start.1 = (f32[2,1,16,320]{3,2,1,0:T(8,128)S(1)}, f32[2,1,16,320]{3,2,1,0:T(8,128)S(1)}, u32[]{:S(2)}, u32[]{:S(2)}) collective-permute-start(f32[2,1,16,320]{3,2,1,0:T(8,128)S(1)} %slice.1140), channel_id=1, source_target_pairs={{0,16},{16,32},{32,48},{48,64},{64,80},{80,96},{96,112},{1,17},{17... | collective-permute-start | bytes 122888 | tf_op jit(solution)/shard_map/ppermute | solution.py:13
  39.2 1.7 collective-permute-done.1
  43.4 4.5 %collective-permute-done.2 = f32[2,1,16,320]{3,2,1,0:T(8,128)S(1)} collective-permute-done((f32[2,1,16,320]{3,2,1,0:T(8,128)S(1)}, f32[2,1,16,320]{3,2,1,0:T(8,128)S(1)}, u32[]{:S(2)}, u32[]{:S(2)}) %collective-permute-start.2) | collective-permute-done | bytes 40992 | tf_op jit(solution)/shard_map/ppermute | solution.py:13
  48.6 3.9 %collective-permute-start.3 = (f32[2,1,16,320]{3,2,1,0:T(8,128)S(1)}, f32[2,1,16,320]{3,2,1,0:T(8,128)S(1)}, u32[]{:S(2)}, u32[]{:S(2)}) collective-permute-start(f32[2,1,16,320]{3,2,1,0:T(8,128)S(1)} %slice.1164), channel_id=1, source_target_pairs={{0,16},{16,32},{32,48},{48,64},{64,80},{80,96},{96,112},{1,17},{17... | collective-permute-start | bytes 122888 | tf_op jit(solution)/shard_map/ppermute | solution.py:13
  52.6 1.7 collective-permute-done.3
  56.9 7.5 %collective-permute-done.4 = f32[2,1,16,320]{3,2,1,0:T(8,128)S(1)} collective-permute-done((f32[2,1,16,320]{3,2,1,0:T(8,128)S(1)}, f32[2,1,16,320]{3,2,1,0:T(8,128)S(1)}, u32[]{:S(2)}, u32[]{:S(2)}) %collective-permute-start.4) | collective-permute-done | bytes 40992 | tf_op jit(solution)/shard_map/ppermute | solution.py:13
  65.2 7.9 %collective-permute-start.5 = (f32[2,1,16,320]{3,2,1,0:T(8,128)S(1)}, f32[2,1,16,320]{3,2,1,0:T(8,128)S(1)}, u32[]{:S(2)}, u32[]{:S(2)}) collective-permute-start(f32[2,1,16,320]{3,2,1,0:T(8,128)S(1)} %slice.1188), channel_id=1, source_target_pairs={{0,16},{16,32},{32,48},{48,64},{64,80},{80,96},{96,112},{1,17},{17... | collective-permute-start | bytes 122888 | tf_op jit(solution)/shard_map/ppermute | solution.py:13
  73.1 1.7 collective-permute-done.5
  77.5 4.5 %collective-permute-done.6 = f32[2,1,16,320]{3,2,1,0:T(8,128)S(1)} collective-permute-done((f32[2,1,16,320]{3,2,1,0:T(8,128)S(1)}, f32[2,1,16,320]{3,2,1,0:T(8,128)S(1)}, u32[]{:S(2)}, u32[]{:S(2)}) %collective-permute-start.6) | collective-permute-done | bytes 40992 | tf_op jit(solution)/shard_map/ppermute | solution.py:13
  82.9 7.5 %collective-permute-start.7 = (f32[2,1,16,320]{3,2,1,0:T(8,128)S(1)}, f32[2,1,16,320]{3,2,1,0:T(8,128)S(1)}, u32[]{:S(2)}, u32[]{:S(2)}) collective-permute-start(f32[2,1,16,320]{3,2,1,0:T(8,128)S(1)} %slice.1212), channel_id=1, source_target_pairs={{0,16},{16,32},{32,48},{48,64},{64,80},{80,96},{96,112},{1,17},{17... | collective-permute-start | bytes 122888 | tf_op jit(solution)/shard_map/ppermute | solution.py:13
  90.5 1.7 collective-permute-done.7
  95.0 4.5 %collective-permute-done.8 = f32[2,1,16,320]{3,2,1,0:T(8,128)S(1)} collective-permute-done((f32[2,1,16,320]{3,2,1,0:T(8,128)S(1)}, f32[2,1,16,320]{3,2,1,0:T(8,128)S(1)}, u32[]{:S(2)}, u32[]{:S(2)}) %collective-permute-start.8) | collective-permute-done | bytes 40992 | tf_op jit(solution)/shard_map/ppermute | solution.py:13
  100.4 7.5 %collective-permute-start.9 = (f32[2,1,16,320]{3,2,1,0:T(8,128)S(1)}, f32[2,1,16,320]{3,2,1,0:T(8,128)S(1)}, u32[]{:S(2)}, u32[]{:S(2)}) collective-permute-start(f32[2,1,16,320]{3,2,1,0:T(8,128)S(1)} %slice.1236), channel_id=1, source_target_pairs={{0,16},{16,32},{32,48},{48,64},{64,80},{80,96},{96,112},{1,17},{17... | collective-permute-start | bytes 122888 | tf_op jit(solution)/shard_map/ppermute | solution.py:13
  108.0 1.7 collective-permute-done.9
  112.8 4.4 %collective-permute-done.10 = f32[2,1,16,320]{3,2,1,0:T(8,128)S(1)} collective-permute-done((f32[2,1,16,320]{3,2,1,0:T(8,128)S(1)}, f32[2,1,16,320]{3,2,1,0:T(8,128)S(1)}, u32[]{:S(2)}, u32[]{:S(2)}) %collective-permute-start.10) | collective-permute-done | bytes 40992 | tf_op jit(solution)/shard_map/ppermute | solution.py:13
  118.2 7.5 %collective-permute-start.11 = (f32[2,1,16,320]{3,2,1,0:T(8,128)S(1)}, f32[2,1,16,320]{3,2,1,0:T(8,128)S(1)}, u32[]{:S(2)}, u32[]{:S(2)}) collective-permute-start(f32[2,1,16,320]{3,2,1,0:T(8,128)S(1)} %slice.1260), channel_id=1, source_target_pairs={{0,16},{16,32},{32,48},{48,64},{64,80},{80,96},{96,112},{1,17},{17... | collective-permute-start | bytes 122888 | tf_op jit(solution)/shard_map/ppermute | solution.py:13
  125.8 1.7 collective-permute-done.11
  130.9 4.5 %collective-permute-done.12 = f32[2,1,16,320]{3,2,1,0:T(8,128)S(1)} collective-permute-done((f32[2,1,16,320]{3,2,1,0:T(8,128)S(1)}, f32[2,1,16,320]{3,2,1,0:T(8,128)S(1)}, u32[]{:S(2)}, u32[]{:S(2)}) %collective-permute-start.12) | collective-permute-done | bytes 40992 | tf_op jit(solution)/shard_map/ppermute | solution.py:13
  137.0 7.5 %collective-permute-start.13 = (f32[2,1,16,320]{3,2,1,0:T(8,128)S(1)}, f32[2,1,16,320]{3,2,1,0:T(8,128)S(1)}, u32[]{:S(2)}, u32[]{:S(2)}) collective-permute-start(f32[2,1,16,320]{3,2,1,0:T(8,128)S(1)} %slice.1284), channel_id=1, source_target_pairs={{0,16},{16,32},{32,48},{48,64},{64,80},{80,96},{96,112},{1,17},{17... | collective-permute-start | bytes 122888 | tf_op jit(solution)/shard_map/ppermute | solution.py:13
  144.6 1.7 collective-permute-done.13
  148.9 4.5 %collective-permute-done.14 = f32[2,1,16,320]{3,2,1,0:T(8,128)S(1)} collective-permute-done((f32[2,1,16,320]{3,2,1,0:T(8,128)S(1)}, f32[2,1,16,320]{3,2,1,0:T(8,128)S(1)}, u32[]{:S(2)}, u32[]{:S(2)}) %collective-permute-start.14) | collective-permute-done | bytes 40992 | tf_op jit(solution)/shard_map/ppermute | solution.py:13
  154.1 7.5 %collective-permute-start.15 = (f32[2,1,16,320]{3,2,1,0:T(8,128)S(1)}, f32[2,1,16,320]{3,2,1,0:T(8,128)S(1)}, u32[]{:S(2)}, u32[]{:S(2)}) collective-permute-start(f32[2,1,16,320]{3,2,1,0:T(8,128)S(1)} %slice.1308), channel_id=1, source_target_pairs={{0,16},{16,32},{32,48},{48,64},{64,80},{80,96},{96,112},{1,17},{17... | collective-permute-start | bytes 122888 | tf_op jit(solution)/shard_map/ppermute | solution.py:13
  161.7 1.7 collective-permute-done.15
  166.3 4.7 %collective-permute-done.16 = f32[2,1,16,320]{3,2,1,0:T(8,128)S(1)} collective-permute-done((f32[2,1,16,320]{3,2,1,0:T(8,128)S(1)}, f32[2,1,16,320]{3,2,1,0:T(8,128)S(1)}, u32[]{:S(2)}, u32[]{:S(2)}) %collective-permute-start.16) | collective-permute-done | bytes 40992 | tf_op jit(solution)/shard_map/ppermute | solution.py:13
  171.7 8.0 %collective-permute-start.17 = (f32[2,1,16,320]{3,2,1,0:T(8,128)S(1)}, f32[2,1,16,320]{3,2,1,0:T(8,128)S(1)}, u32[]{:S(2)}, u32[]{:S(2)}) collective-permute-start(f32[2,1,16,320]{3,2,1,0:T(8,128)S(1)} %slice.1332), channel_id=1, source_target_pairs={{0,16},{16,32},{32,48},{48,64},{64,80},{80,96},{96,112},{1,17},{17... | collective-permute-start | bytes 122888 | tf_op jit(solution)/shard_map/ppermute | solution.py:13
  184.1 4.5 %collective-permute-done.18 = f32[2,1,16,320]{3,2,1,0:T(8,128)S(1)} collective-permute-done((f32[2,1,16,320]{3,2,1,0:T(8,128)S(1)}, f32[2,1,16,320]{3,2,1,0:T(8,128)S(1)}, u32[]{:S(2)}, u32[]{:S(2)}) %collective-permute-start.18) | collective-permute-done | bytes 40992 | tf_op jit(solution)/shard_map/ppermute | solution.py:13
  189.4 7.5 %collective-permute-start.19 = (f32[2,1,16,320]{3,2,1,0:T(8,128)S(1)}, f32[2,1,16,320]{3,2,1,0:T(8,128)S(1)}, u32[]{:S(2)}, u32[]{:S(2)}) collective-permute-start(f32[2,1,16,320]{3,2,1,0:T(8,128)S(1)} %slice.1356), channel_id=1, source_target_pairs={{0,16},{16,32},{32,48},{48,64},{64,80},{80,96},{96,112},{1,17},{17... | collective-permute-start | bytes 122888 | tf_op jit(solution)/shard_map/ppermute | solution.py:13
  201.2 4.5 %collective-permute-done.20 = f32[2,1,16,320]{3,2,1,0:T(8,128)S(1)} collective-permute-done((f32[2,1,16,320]{3,2,1,0:T(8,128)S(1)}, f32[2,1,16,320]{3,2,1,0:T(8,128)S(1)}, u32[]{:S(2)}, u32[]{:S(2)}) %collective-permute-start.20) | collective-permute-done | bytes 40992 | tf_op jit(solution)/shard_map/ppermute | solution.py:13
  206.7 7.5 %collective-permute-start.21 = (f32[2,1,16,320]{3,2,1,0:T(8,128)S(1)}, f32[2,1,16,320]{3,2,1,0:T(8,128)S(1)}, u32[]{:S(2)}, u32[]{:S(2)}) collective-permute-start(f32[2,1,16,320]{3,2,1,0:T(8,128)S(1)} %slice.1380), channel_id=1, source_target_pairs={{0,16},{16,32},{32,48},{48,64},{64,80},{80,96},{96,112},{1,17},{17... | collective-permute-start | bytes 122888 | tf_op jit(solution)/shard_map/ppermute | solution.py:13
  218.0 3.7 %fusion.6 = f32[1,3,16,16,320]{4,3,2,1,0:T(8,128)} fusion(f32[1,3,16,16,320]{4,3,2,1,0:T(8,128)S(1)} %copy-done, f32[1,1,16,16,320]{4,3,2,1,0:T(8,128)S(1)} %bitcast.800, f32[1,1,16,16,320]{4,3,2,1,0:T(8,128)S(1)} %bitcast.807, f32[1,1,16,16,320]{4,3,2,1,0:T(8,128)S(1)} %bitcast.793, f32[1,1,16,16,320]{4,3,2,1,0:T(8,128)S(1)} %bitcast.819, ...), kind=kLoop, calls=%fused_computation.8 | loop fusion | flops 5898240 | bytes 8192000 | tf_op jit(solution)/shard_map/add | solution.py:70
  221.7 62.3 %reduce-scatter.2.cloned.1.call-done = f32[1,16,320]{2,1,0:T(8,128)} async-done(((f32[16,16,320]{2,1,0:T(8,128)}), f32[1,16,320]{2,1,0:T(8,128)}) %reduce-scatter.2.cloned.1.call-update) | async-done | bytes 20496 | tf_op jit(solution)/shard_map/reduce_scatter | solution.py:57
  (232 shorter events, 50.3 us)
Async XLA Ops:
  7.2 276.9 %reduce-scatter.2.cloned.1.call-start = ((), (), s32[]{:S(2)}) async-start(), calls=%async_computation.1 | async-start | bytes 417792 | tf_op jit(solution)/shard_map/reduce_scatter | solution.py:57
  8.0 25.0 %collective-permute-start = (f32[2,1,16,320]{3,2,1,0:T(8,128)S(1)}, f32[2,1,16,320]{3,2,1,0:T(8,128)S(1)}, u32[]{:S(2)}, u32[]{:S(2)}) collective-permute-start(f32[2,1,16,320]{3,2,1,0:T(8,128)S(1)} %slice.1129), channel_id=1, source_target_pairs={{16,0},{32,16},{48,32},{64,48},{80,64},{96,80},{112,96},{17,1},{33... | collective-permute-start | bytes 122888 | tf_op jit(solution)/shard_map/ppermute | solution.py:13
  32.6 77.6 %copy-start.3 = (f32[16,16,320]{2,1,0:T(8,128)}, f32[16,16,320]{2,1,0:T(8,128)S(1)}, u32[]{:S(2)}) copy-start(f32[16,16,320]{2,1,0:T(8,128)S(1)} %get-tuple-element.191) | copy-start | bytes 983044
  34.6 6.3 %collective-permute-start.1 = (f32[2,1,16,320]{3,2,1,0:T(8,128)S(1)}, f32[2,1,16,320]{3,2,1,0:T(8,128)S(1)}, u32[]{:S(2)}, u32[]{:S(2)}) collective-permute-start(f32[2,1,16,320]{3,2,1,0:T(8,128)S(1)} %slice.1140), channel_id=1, source_target_pairs={{0,16},{16,32},{32,48},{48,64},{64,80},{80,96},{96,112},{1,17},{17... | collective-permute-start | bytes 122888 | tf_op jit(solution)/shard_map/ppermute | solution.py:13
  41.7 6.3 %collective-permute-start.2 = (f32[2,1,16,320]{3,2,1,0:T(8,128)S(1)}, f32[2,1,16,320]{3,2,1,0:T(8,128)S(1)}, u32[]{:S(2)}, u32[]{:S(2)}) collective-permute-start(f32[2,1,16,320]{3,2,1,0:T(8,128)S(1)} %slice.1153), channel_id=1, source_target_pairs={{16,0},{32,16},{48,32},{64,48},{80,64},{96,80},{112,96},{17,1},{33... | collective-permute-start | bytes 122888 | tf_op jit(solution)/shard_map/ppermute | solution.py:13
  48.6 5.7 %collective-permute-start.3 = (f32[2,1,16,320]{3,2,1,0:T(8,128)S(1)}, f32[2,1,16,320]{3,2,1,0:T(8,128)S(1)}, u32[]{:S(2)}, u32[]{:S(2)}) collective-permute-start(f32[2,1,16,320]{3,2,1,0:T(8,128)S(1)} %slice.1164), channel_id=1, source_target_pairs={{0,16},{16,32},{32,48},{48,64},{64,80},{80,96},{96,112},{1,17},{17... | collective-permute-start | bytes 122888 | tf_op jit(solution)/shard_map/ppermute | solution.py:13
  55.1 9.3 %collective-permute-start.4 = (f32[2,1,16,320]{3,2,1,0:T(8,128)S(1)}, f32[2,1,16,320]{3,2,1,0:T(8,128)S(1)}, u32[]{:S(2)}, u32[]{:S(2)}) collective-permute-start(f32[2,1,16,320]{3,2,1,0:T(8,128)S(1)} %slice.1177), channel_id=1, source_target_pairs={{16,0},{32,16},{48,32},{64,48},{80,64},{96,80},{112,96},{17,1},{33... | collective-permute-start | bytes 122888 | tf_op jit(solution)/shard_map/ppermute | solution.py:13
  65.2 9.6 %collective-permute-start.5 = (f32[2,1,16,320]{3,2,1,0:T(8,128)S(1)}, f32[2,1,16,320]{3,2,1,0:T(8,128)S(1)}, u32[]{:S(2)}, u32[]{:S(2)}) collective-permute-start(f32[2,1,16,320]{3,2,1,0:T(8,128)S(1)} %slice.1188), channel_id=1, source_target_pairs={{0,16},{16,32},{32,48},{48,64},{64,80},{80,96},{96,112},{1,17},{17... | collective-permute-start | bytes 122888 | tf_op jit(solution)/shard_map/ppermute | solution.py:13
  75.3 141.1 %copy-start.4 = (f32[16,16,320]{2,1,0:T(8,128)}, f32[16,16,320]{2,1,0:T(8,128)S(1)}, u32[]{:S(2)}) copy-start(f32[16,16,320]{2,1,0:T(8,128)S(1)} %get-tuple-element.142) | copy-start | bytes 983044
  75.3 141.1 %copy-start.5 = (f32[16,16,320]{2,1,0:T(8,128)}, f32[16,16,320]{2,1,0:T(8,128)S(1)}, u32[]{:S(2)}) copy-start(f32[16,16,320]{2,1,0:T(8,128)S(1)} %get-tuple-element.143) | copy-start | bytes 983044
  75.3 141.1 %copy-start.6 = (f32[16,16,320]{2,1,0:T(8,128)}, f32[16,16,320]{2,1,0:T(8,128)S(1)}, u32[]{:S(2)}) copy-start(f32[16,16,320]{2,1,0:T(8,128)S(1)} %get-tuple-element.144) | copy-start | bytes 983044
  75.8 6.3 %collective-permute-start.6 = (f32[2,1,16,320]{3,2,1,0:T(8,128)S(1)}, f32[2,1,16,320]{3,2,1,0:T(8,128)S(1)}, u32[]{:S(2)}, u32[]{:S(2)}) collective-permute-start(f32[2,1,16,320]{3,2,1,0:T(8,128)S(1)} %slice.1201), channel_id=1, source_target_pairs={{16,0},{32,16},{48,32},{64,48},{80,64},{96,80},{112,96},{17,1},{33... | collective-permute-start | bytes 122888 | tf_op jit(solution)/shard_map/ppermute | solution.py:13
  82.9 9.3 %collective-permute-start.7 = (f32[2,1,16,320]{3,2,1,0:T(8,128)S(1)}, f32[2,1,16,320]{3,2,1,0:T(8,128)S(1)}, u32[]{:S(2)}, u32[]{:S(2)}) collective-permute-start(f32[2,1,16,320]{3,2,1,0:T(8,128)S(1)} %slice.1212), channel_id=1, source_target_pairs={{0,16},{16,32},{32,48},{48,64},{64,80},{80,96},{96,112},{1,17},{17... | collective-permute-start | bytes 122888 | tf_op jit(solution)/shard_map/ppermute | solution.py:13
  92.6 71.3 %copy-start.7 = (f32[16,16,320]{2,1,0:T(8,128)}, f32[16,16,320]{2,1,0:T(8,128)S(1)}, u32[]{:S(2)}) copy-start(f32[16,16,320]{2,1,0:T(8,128)S(1)} %get-tuple-element.126) | copy-start | bytes 983044
  92.7 71.3 %copy-start.8 = (f32[16,16,320]{2,1,0:T(8,128)}, f32[16,16,320]{2,1,0:T(8,128)S(1)}, u32[]{:S(2)}) copy-start(f32[16,16,320]{2,1,0:T(8,128)S(1)} %get-tuple-element.127) | copy-start | bytes 983044
  92.7 71.3 %copy-start.9 = (f32[16,16,320]{2,1,0:T(8,128)}, f32[16,16,320]{2,1,0:T(8,128)S(1)}, u32[]{:S(2)}) copy-start(f32[16,16,320]{2,1,0:T(8,128)S(1)} %get-tuple-element.128) | copy-start | bytes 983044
  93.2 6.3 %collective-permute-start.8 = (f32[2,1,16,320]{3,2,1,0:T(8,128)S(1)}, f32[2,1,16,320]{3,2,1,0:T(8,128)S(1)}, u32[]{:S(2)}, u32[]{:S(2)}) collective-permute-start(f32[2,1,16,320]{3,2,1,0:T(8,128)S(1)} %slice.1225), channel_id=1, source_target_pairs={{16,0},{32,16},{48,32},{64,48},{80,64},{96,80},{112,96},{17,1},{33... | collective-permute-start | bytes 122888 | tf_op jit(solution)/shard_map/ppermute | solution.py:13
  100.4 9.3 %collective-permute-start.9 = (f32[2,1,16,320]{3,2,1,0:T(8,128)S(1)}, f32[2,1,16,320]{3,2,1,0:T(8,128)S(1)}, u32[]{:S(2)}, u32[]{:S(2)}) collective-permute-start(f32[2,1,16,320]{3,2,1,0:T(8,128)S(1)} %slice.1236), channel_id=1, source_target_pairs={{0,16},{16,32},{32,48},{48,64},{64,80},{80,96},{96,112},{1,17},{17... | collective-permute-start | bytes 122888 | tf_op jit(solution)/shard_map/ppermute | solution.py:13
  110.1 53.8 %copy-start.10 = (f32[16,16,320]{2,1,0:T(8,128)}, f32[16,16,320]{2,1,0:T(8,128)S(1)}, u32[]{:S(2)}) copy-start(f32[16,16,320]{2,1,0:T(8,128)S(1)} %get-tuple-element.110) | copy-start | bytes 983044
  110.1 53.8 %copy-start.11 = (f32[16,16,320]{2,1,0:T(8,128)}, f32[16,16,320]{2,1,0:T(8,128)S(1)}, u32[]{:S(2)}) copy-start(f32[16,16,320]{2,1,0:T(8,128)S(1)} %get-tuple-element.111) | copy-start | bytes 983044
  110.8 6.3 %collective-permute-start.10 = (f32[2,1,16,320]{3,2,1,0:T(8,128)S(1)}, f32[2,1,16,320]{3,2,1,0:T(8,128)S(1)}, u32[]{:S(2)}, u32[]{:S(2)}) collective-permute-start(f32[2,1,16,320]{3,2,1,0:T(8,128)S(1)} %slice.1249), channel_id=1, source_target_pairs={{16,0},{32,16},{48,32},{64,48},{80,64},{96,80},{112,96},{17,1},{33... | collective-permute-start | bytes 122888 | tf_op jit(solution)/shard_map/ppermute | solution.py:13
  118.2 9.3 %collective-permute-start.11 = (f32[2,1,16,320]{3,2,1,0:T(8,128)S(1)}, f32[2,1,16,320]{3,2,1,0:T(8,128)S(1)}, u32[]{:S(2)}, u32[]{:S(2)}) collective-permute-start(f32[2,1,16,320]{3,2,1,0:T(8,128)S(1)} %slice.1260), channel_id=1, source_target_pairs={{0,16},{16,32},{32,48},{48,64},{64,80},{80,96},{96,112},{1,17},{17... | collective-permute-start | bytes 122888 | tf_op jit(solution)/shard_map/ppermute | solution.py:13
  129.1 6.3 %collective-permute-start.12 = (f32[2,1,16,320]{3,2,1,0:T(8,128)S(1)}, f32[2,1,16,320]{3,2,1,0:T(8,128)S(1)}, u32[]{:S(2)}, u32[]{:S(2)}) collective-permute-start(f32[2,1,16,320]{3,2,1,0:T(8,128)S(1)} %slice.1273), channel_id=1, source_target_pairs={{16,0},{32,16},{48,32},{64,48},{80,64},{96,80},{112,96},{17,1},{33... | collective-permute-start | bytes 122888 | tf_op jit(solution)/shard_map/ppermute | solution.py:13
  137.0 9.3 %collective-permute-start.13 = (f32[2,1,16,320]{3,2,1,0:T(8,128)S(1)}, f32[2,1,16,320]{3,2,1,0:T(8,128)S(1)}, u32[]{:S(2)}, u32[]{:S(2)}) collective-permute-start(f32[2,1,16,320]{3,2,1,0:T(8,128)S(1)} %slice.1284), channel_id=1, source_target_pairs={{0,16},{16,32},{32,48},{48,64},{64,80},{80,96},{96,112},{1,17},{17... | collective-permute-start | bytes 122888 | tf_op jit(solution)/shard_map/ppermute | solution.py:13
  147.1 6.3 %collective-permute-start.14 = (f32[2,1,16,320]{3,2,1,0:T(8,128)S(1)}, f32[2,1,16,320]{3,2,1,0:T(8,128)S(1)}, u32[]{:S(2)}, u32[]{:S(2)}) collective-permute-start(f32[2,1,16,320]{3,2,1,0:T(8,128)S(1)} %slice.1297), channel_id=1, source_target_pairs={{16,0},{32,16},{48,32},{64,48},{80,64},{96,80},{112,96},{17,1},{33... | collective-permute-start | bytes 122888 | tf_op jit(solution)/shard_map/ppermute | solution.py:13
  154.1 9.3 %collective-permute-start.15 = (f32[2,1,16,320]{3,2,1,0:T(8,128)S(1)}, f32[2,1,16,320]{3,2,1,0:T(8,128)S(1)}, u32[]{:S(2)}, u32[]{:S(2)}) collective-permute-start(f32[2,1,16,320]{3,2,1,0:T(8,128)S(1)} %slice.1308), channel_id=1, source_target_pairs={{0,16},{16,32},{32,48},{48,64},{64,80},{80,96},{96,112},{1,17},{17... | collective-permute-start | bytes 122888 | tf_op jit(solution)/shard_map/ppermute | solution.py:13
  164.5 6.5 %collective-permute-start.16 = (f32[2,1,16,320]{3,2,1,0:T(8,128)S(1)}, f32[2,1,16,320]{3,2,1,0:T(8,128)S(1)}, u32[]{:S(2)}, u32[]{:S(2)}) collective-permute-start(f32[2,1,16,320]{3,2,1,0:T(8,128)S(1)} %slice.1321), channel_id=1, source_target_pairs={{16,0},{32,16},{48,32},{64,48},{80,64},{96,80},{112,96},{17,1},{33... | collective-permute-start | bytes 122888 | tf_op jit(solution)/shard_map/ppermute | solution.py:13
  171.7 9.7 %collective-permute-start.17 = (f32[2,1,16,320]{3,2,1,0:T(8,128)S(1)}, f32[2,1,16,320]{3,2,1,0:T(8,128)S(1)}, u32[]{:S(2)}, u32[]{:S(2)}) collective-permute-start(f32[2,1,16,320]{3,2,1,0:T(8,128)S(1)} %slice.1332), channel_id=1, source_target_pairs={{0,16},{16,32},{32,48},{48,64},{64,80},{80,96},{96,112},{1,17},{17... | collective-permute-start | bytes 122888 | tf_op jit(solution)/shard_map/ppermute | solution.py:13
  182.3 6.3 %collective-permute-start.18 = (f32[2,1,16,320]{3,2,1,0:T(8,128)S(1)}, f32[2,1,16,320]{3,2,1,0:T(8,128)S(1)}, u32[]{:S(2)}, u32[]{:S(2)}) collective-permute-start(f32[2,1,16,320]{3,2,1,0:T(8,128)S(1)} %slice.1345), channel_id=1, source_target_pairs={{16,0},{32,16},{48,32},{64,48},{80,64},{96,80},{112,96},{17,1},{33... | collective-permute-start | bytes 122888 | tf_op jit(solution)/shard_map/ppermute | solution.py:13
  189.4 9.3 %collective-permute-start.19 = (f32[2,1,16,320]{3,2,1,0:T(8,128)S(1)}, f32[2,1,16,320]{3,2,1,0:T(8,128)S(1)}, u32[]{:S(2)}, u32[]{:S(2)}) collective-permute-start(f32[2,1,16,320]{3,2,1,0:T(8,128)S(1)} %slice.1356), channel_id=1, source_target_pairs={{0,16},{16,32},{32,48},{48,64},{64,80},{80,96},{96,112},{1,17},{17... | collective-permute-start | bytes 122888 | tf_op jit(solution)/shard_map/ppermute | solution.py:13
  199.5 6.3 %collective-permute-start.20 = (f32[2,1,16,320]{3,2,1,0:T(8,128)S(1)}, f32[2,1,16,320]{3,2,1,0:T(8,128)S(1)}, u32[]{:S(2)}, u32[]{:S(2)}) collective-permute-start(f32[2,1,16,320]{3,2,1,0:T(8,128)S(1)} %slice.1369), channel_id=1, source_target_pairs={{16,0},{32,16},{48,32},{64,48},{80,64},{96,80},{112,96},{17,1},{33... | collective-permute-start | bytes 122888 | tf_op jit(solution)/shard_map/ppermute | solution.py:13
  206.7 9.3 %collective-permute-start.21 = (f32[2,1,16,320]{3,2,1,0:T(8,128)S(1)}, f32[2,1,16,320]{3,2,1,0:T(8,128)S(1)}, u32[]{:S(2)}, u32[]{:S(2)}) collective-permute-start(f32[2,1,16,320]{3,2,1,0:T(8,128)S(1)} %slice.1380), channel_id=1, source_target_pairs={{0,16},{16,32},{32,48},{48,64},{64,80},{80,96},{96,112},{1,17},{17... | collective-permute-start | bytes 122888 | tf_op jit(solution)/shard_map/ppermute | solution.py:13
  (9 other events, 85.2 us)
Sparse Core Ops, SparseCore 0:
  218.2 65.8 reduce-scatter.1
where the time goes:
time: 293 us; the launch traced here: 292 us
  waiting for transfers between devices  129 us (44%)
  starting transfers between devices  91.6 us (31%)
  other arithmetic  22 us (8%)
  blocking collectives  21.7 us (7%)
  between operations  15.5 us (5%)
  local copies, waits for them, and re-layouts  12.3 us (4%)
    ppermute x22, starting transfers between devices, passed_along(): return lax.ppermute(array, axis, pairs)  91.6 us
    ppermute x22, waiting for transfers between devices, passed_along(): return lax.ppermute(array, axis, pairs)  66.7 us
    reduce_scatter x1, waiting for transfers between devices, add_term(): lax.psum_scatter(term, 'src', scatter_dimension=0, tiled=True)  62.3 us
    all_gather x1, blocking collectives, on_device(): window = lax.all_gather(permittivity, 'src', axis=0, tiled=True)  21.7 us
  transfers between devices with their start and end apart: 23, of which 22 were waited for; matrix products, arithmetic and copies ran while one was open for 4% of the time, Pallas kernels for 0%

commit v1 on v0

--- a/solution.py
+++ b/solution.py
@@ -59,7 +59,8 @@
 
 
 def on_device(permittivity, e_start, h_start, e_cotangent, h_cotangent):
-    window = lax.all_gather(permittivity, "src", axis=0, tiled=True)
+    stack = jnp.stack([permittivity] * lax.axis_size("src"))
+    window = jnp.concatenate(lax.all_to_all(stack, "src", 0, 0), axis=0)
     inverse = 1.0 / window
     efield = e_start[0]
     hfield = h_start[0]

time: 293 us -> 283 us (0.966)
  blocking collectives: 21.7 us -> 0 us
  starting transfers between devices: 91.6 us -> 97.1 us
    all_gather x1 -> x0, blocking collectives: 21.7 us -> none  [on_device(): window = lax.all_gather(permittivity, 'src', axis=0, tiled=True)]
    all_to_all x0 -> x1, starting transfers between devices: none -> 5.66 us  [on_device(): window = jnp.concatenate(lax.all_to_all(stack, 'src', 0, 0), axis=0)]
  transfers between devices with their start and end apart: 23 -> 24, of which waited for: 22 -> 23; matrix products, arithmetic and copies ran while one was open for 4% -> 4% of each run, Pallas kernels for 0% -> 0%
where the time goes in v1:
time: 283 us; the launch traced here: 282 us
  waiting for transfers between devices  131 us (46%)
  starting transfers between devices  97.1 us (34%)
  other arithmetic  24 us (8%)
  between operations  15.7 us (6%)
  local copies, waits for them, and re-layouts  14.2 us (5%)
    ppermute x22, starting transfers between devices, passed_along(): return lax.ppermute(array, axis, pairs)  91.4 us
    ppermute x22, waiting for transfers between devices, passed_along(): return lax.ppermute(array, axis, pairs)  65.4 us
    reduce_scatter x1, waiting for transfers between devices, add_term(): lax.psum_scatter(term, 'src', scatter_dimension=0, tiled=True)  64.9 us
  transfers between devices with their start and end apart: 24, of which 23 were waited for; matrix products, arithmetic and copies ran while one was open for 4% of the time, Pallas kernels for 0%

profile of v1, /device:TPU:0, one launch (start us, length us, event | category | flops | bytes accessed | tf_op | source)
XLA Modules:
  0.0 281.7 jit_solution(14012545013130391032)
XLA Ops:
  10.9 5.7 %all-to-all-start = ((f32[16,1,16,320]{3,2,1,0:T(8,128)}), f32[16,1,16,320]{3,2,1,0:T(8,128)}, u32[]{:S(2)}, u32[]{:S(2)}) async-start(f32[16,1,16,320]{3,2,1,0:T(8,128)} %stack.331), calls=%async_computation | async-start | bytes 786432 | tf_op jit(solution)/shard_map/all_to_all | solution.py:63
  18.9 4.5 %collective-permute-start.1 = (f32[2,1,16,320]{3,2,1,0:T(8,128)S(1)}, f32[2,1,16,320]{3,2,1,0:T(8,128)S(1)}, u32[]{:S(2)}, u32[]{:S(2)}) collective-permute-start(f32[2,1,16,320]{3,2,1,0:T(8,128)S(1)} %slice.1140), channel_id=1, source_target_pairs={{0,16},{16,32},{32,48},{48,64},{64,80},{80,96},{96,112},{1,17},{17... | collective-permute-start | bytes 122888 | tf_op jit(solution)/shard_map/ppermute | solution.py:13
  23.5 1.7 collective-permute-done.1
  30.2 3.8 %collective-permute-done.2 = f32[2,1,16,320]{3,2,1,0:T(8,128)S(1)} collective-permute-done((f32[2,1,16,320]{3,2,1,0:T(8,128)S(1)}, f32[2,1,16,320]{3,2,1,0:T(8,128)S(1)}, u32[]{:S(2)}, u32[]{:S(2)}) %collective-permute-start.2) | collective-permute-done | bytes 40992 | tf_op jit(solution)/shard_map/ppermute | solution.py:13
  35.6 3.9 %collective-permute-start.3 = (f32[2,1,16,320]{3,2,1,0:T(8,128)S(1)}, f32[2,1,16,320]{3,2,1,0:T(8,128)S(1)}, u32[]{:S(2)}, u32[]{:S(2)}) collective-permute-start(f32[2,1,16,320]{3,2,1,0:T(8,128)S(1)} %slice.1164), channel_id=1, source_target_pairs={{0,16},{16,32},{32,48},{48,64},{64,80},{80,96},{96,112},{1,17},{17... | collective-permute-start | bytes 122888 | tf_op jit(solution)/shard_map/ppermute | solution.py:13
  39.6 1.7 collective-permute-done.3
  44.0 6.9 %collective-permute-done.4 = f32[2,1,16,320]{3,2,1,0:T(8,128)S(1)} collective-permute-done((f32[2,1,16,320]{3,2,1,0:T(8,128)S(1)}, f32[2,1,16,320]{3,2,1,0:T(8,128)S(1)}, u32[]{:S(2)}, u32[]{:S(2)}) %collective-permute-start.4) | collective-permute-done | bytes 40992 | tf_op jit(solution)/shard_map/ppermute | solution.py:13
  51.6 7.9 %collective-permute-start.5 = (f32[2,1,16,320]{3,2,1,0:T(8,128)S(1)}, f32[2,1,16,320]{3,2,1,0:T(8,128)S(1)}, u32[]{:S(2)}, u32[]{:S(2)}) collective-permute-start(f32[2,1,16,320]{3,2,1,0:T(8,128)S(1)} %slice.1188), channel_id=1, source_target_pairs={{0,16},{16,32},{32,48},{48,64},{64,80},{80,96},{96,112},{1,17},{17... | collective-permute-start | bytes 122888 | tf_op jit(solution)/shard_map/ppermute | solution.py:13
  59.6 1.7 collective-permute-done.5
  64.0 4.5 %collective-permute-done.6 = f32[2,1,16,320]{3,2,1,0:T(8,128)S(1)} collective-permute-done((f32[2,1,16,320]{3,2,1,0:T(8,128)S(1)}, f32[2,1,16,320]{3,2,1,0:T(8,128)S(1)}, u32[]{:S(2)}, u32[]{:S(2)}) %collective-permute-start.6) | collective-permute-done | bytes 40992 | tf_op jit(solution)/shard_map/ppermute | solution.py:13
  69.3 7.5 %collective-permute-start.7 = (f32[2,1,16,320]{3,2,1,0:T(8,128)S(1)}, f32[2,1,16,320]{3,2,1,0:T(8,128)S(1)}, u32[]{:S(2)}, u32[]{:S(2)}) collective-permute-start(f32[2,1,16,320]{3,2,1,0:T(8,128)S(1)} %slice.1212), channel_id=1, source_target_pairs={{0,16},{16,32},{32,48},{48,64},{64,80},{80,96},{96,112},{1,17},{17... | collective-permute-start | bytes 122888 | tf_op jit(solution)/shard_map/ppermute | solution.py:13
  76.9 1.7 collective-permute-done.7
  81.4 4.5 %collective-permute-done.8 = f32[2,1,16,320]{3,2,1,0:T(8,128)S(1)} collective-permute-done((f32[2,1,16,320]{3,2,1,0:T(8,128)S(1)}, f32[2,1,16,320]{3,2,1,0:T(8,128)S(1)}, u32[]{:S(2)}, u32[]{:S(2)}) %collective-permute-start.8) | collective-permute-done | bytes 40992 | tf_op jit(solution)/shard_map/ppermute | solution.py:13
  86.9 7.5 %collective-permute-start.9 = (f32[2,1,16,320]{3,2,1,0:T(8,128)S(1)}, f32[2,1,16,320]{3,2,1,0:T(8,128)S(1)}, u32[]{:S(2)}, u32[]{:S(2)}) collective-permute-start(f32[2,1,16,320]{3,2,1,0:T(8,128)S(1)} %slice.1236), channel_id=1, source_target_pairs={{0,16},{16,32},{32,48},{48,64},{64,80},{80,96},{96,112},{1,17},{17... | collective-permute-start | bytes 122888 | tf_op jit(solution)/shard_map/ppermute | solution.py:13
  94.5 1.7 collective-permute-done.9
  99.2 4.4 %collective-permute-done.10 = f32[2,1,16,320]{3,2,1,0:T(8,128)S(1)} collective-permute-done((f32[2,1,16,320]{3,2,1,0:T(8,128)S(1)}, f32[2,1,16,320]{3,2,1,0:T(8,128)S(1)}, u32[]{:S(2)}, u32[]{:S(2)}) %collective-permute-start.10) | collective-permute-done | bytes 40992 | tf_op jit(solution)/shard_map/ppermute | solution.py:13
  104.6 7.5 %collective-permute-start.11 = (f32[2,1,16,320]{3,2,1,0:T(8,128)S(1)}, f32[2,1,16,320]{3,2,1,0:T(8,128)S(1)}, u32[]{:S(2)}, u32[]{:S(2)}) collective-permute-start(f32[2,1,16,320]{3,2,1,0:T(8,128)S(1)} %slice.1260), channel_id=1, source_target_pairs={{0,16},{16,32},{32,48},{48,64},{64,80},{80,96},{96,112},{1,17},{17... | collective-permute-start | bytes 122888 | tf_op jit(solution)/shard_map/ppermute | solution.py:13
  112.2 1.7 collective-permute-done.11
  117.3 4.5 %collective-permute-done.12 = f32[2,1,16,320]{3,2,1,0:T(8,128)S(1)} collective-permute-done((f32[2,1,16,320]{3,2,1,0:T(8,128)S(1)}, f32[2,1,16,320]{3,2,1,0:T(8,128)S(1)}, u32[]{:S(2)}, u32[]{:S(2)}) %collective-permute-start.12) | collective-permute-done | bytes 40992 | tf_op jit(solution)/shard_map/ppermute | solution.py:13
  123.4 7.5 %collective-permute-start.13 = (f32[2,1,16,320]{3,2,1,0:T(8,128)S(1)}, f32[2,1,16,320]{3,2,1,0:T(8,128)S(1)}, u32[]{:S(2)}, u32[]{:S(2)}) collective-permute-start(f32[2,1,16,320]{3,2,1,0:T(8,128)S(1)} %slice.1284), channel_id=1, source_target_pairs={{0,16},{16,32},{32,48},{48,64},{64,80},{80,96},{96,112},{1,17},{17... | collective-permute-start | bytes 122888 | tf_op jit(solution)/shard_map/ppermute | solution.py:13
  135.3 4.5 %collective-permute-done.14 = f32[2,1,16,320]{3,2,1,0:T(8,128)S(1)} collective-permute-done((f32[2,1,16,320]{3,2,1,0:T(8,128)S(1)}, f32[2,1,16,320]{3,2,1,0:T(8,128)S(1)}, u32[]{:S(2)}, u32[]{:S(2)}) %collective-permute-start.14) | collective-permute-done | bytes 40992 | tf_op jit(solution)/shard_map/ppermute | solution.py:13
  140.5 7.5 %collective-permute-start.15 = (f32[2,1,16,320]{3,2,1,0:T(8,128)S(1)}, f32[2,1,16,320]{3,2,1,0:T(8,128)S(1)}, u32[]{:S(2)}, u32[]{:S(2)}) collective-permute-start(f32[2,1,16,320]{3,2,1,0:T(8,128)S(1)} %slice.1308), channel_id=1, source_target_pairs={{0,16},{16,32},{32,48},{48,64},{64,80},{80,96},{96,112},{1,17},{17... | collective-permute-start | bytes 122888 | tf_op jit(solution)/shard_map/ppermute | solution.py:13
  152.7 4.7 %collective-permute-done.16 = f32[2,1,16,320]{3,2,1,0:T(8,128)S(1)} collective-permute-done((f32[2,1,16,320]{3,2,1,0:T(8,128)S(1)}, f32[2,1,16,320]{3,2,1,0:T(8,128)S(1)}, u32[]{:S(2)}, u32[]{:S(2)}) %collective-permute-start.16) | collective-permute-done | bytes 40992 | tf_op jit(solution)/shard_map/ppermute | solution.py:13
  158.1 8.0 %collective-permute-start.17 = (f32[2,1,16,320]{3,2,1,0:T(8,128)S(1)}, f32[2,1,16,320]{3,2,1,0:T(8,128)S(1)}, u32[]{:S(2)}, u32[]{:S(2)}) collective-permute-start(f32[2,1,16,320]{3,2,1,0:T(8,128)S(1)} %slice.1332), channel_id=1, source_target_pairs={{0,16},{16,32},{32,48},{48,64},{64,80},{80,96},{96,112},{1,17},{17... | collective-permute-start | bytes 122888 | tf_op jit(solution)/shard_map/ppermute | solution.py:13
  170.5 4.5 %collective-permute-done.18 = f32[2,1,16,320]{3,2,1,0:T(8,128)S(1)} collective-permute-done((f32[2,1,16,320]{3,2,1,0:T(8,128)S(1)}, f32[2,1,16,320]{3,2,1,0:T(8,128)S(1)}, u32[]{:S(2)}, u32[]{:S(2)}) %collective-permute-start.18) | collective-permute-done | bytes 40992 | tf_op jit(solution)/shard_map/ppermute | solution.py:13
  175.8 7.5 %collective-permute-start.19 = (f32[2,1,16,320]{3,2,1,0:T(8,128)S(1)}, f32[2,1,16,320]{3,2,1,0:T(8,128)S(1)}, u32[]{:S(2)}, u32[]{:S(2)}) collective-permute-start(f32[2,1,16,320]{3,2,1,0:T(8,128)S(1)} %slice.1356), channel_id=1, source_target_pairs={{0,16},{16,32},{32,48},{48,64},{64,80},{80,96},{96,112},{1,17},{17... | collective-permute-start | bytes 122888 | tf_op jit(solution)/shard_map/ppermute | solution.py:13
  183.4 1.7 collective-permute-done.19
  187.6 4.5 %collective-permute-done.20 = f32[2,1,16,320]{3,2,1,0:T(8,128)S(1)} collective-permute-done((f32[2,1,16,320]{3,2,1,0:T(8,128)S(1)}, f32[2,1,16,320]{3,2,1,0:T(8,128)S(1)}, u32[]{:S(2)}, u32[]{:S(2)}) %collective-permute-start.20) | collective-permute-done | bytes 40992 | tf_op jit(solution)/shard_map/ppermute | solution.py:13
  193.1 7.5 %collective-permute-start.21 = (f32[2,1,16,320]{3,2,1,0:T(8,128)S(1)}, f32[2,1,16,320]{3,2,1,0:T(8,128)S(1)}, u32[]{:S(2)}, u32[]{:S(2)}) collective-permute-start(f32[2,1,16,320]{3,2,1,0:T(8,128)S(1)} %slice.1380), channel_id=1, source_target_pairs={{0,16},{16,32},{32,48},{48,64},{64,80},{80,96},{96,112},{1,17},{17... | collective-permute-start | bytes 122888 | tf_op jit(solution)/shard_map/ppermute | solution.py:13
  200.7 1.7 collective-permute-done.21
  204.9 3.7 %fusion.6 = f32[1,3,16,16,320]{4,3,2,1,0:T(8,128)} fusion(f32[1,3,16,16,320]{4,3,2,1,0:T(8,128)S(1)} %copy-done, f32[1,1,16,16,320]{4,3,2,1,0:T(8,128)S(1)} %bitcast.805, f32[1,1,16,16,320]{4,3,2,1,0:T(8,128)S(1)} %bitcast.812, f32[1,1,16,16,320]{4,3,2,1,0:T(8,128)S(1)} %bitcast.798, f32[1,1,16,16,320]{4,3,2,1,0:T(8,128)S(1)} %bitcast.824, ...), kind=kLoop, calls=%fused_computation.8 | loop fusion | flops 5898240 | bytes 8192000 | tf_op jit(solution)/shard_map/add | solution.py:71
  208.6 64.9 %reduce-scatter.2.cloned.1.call-done = f32[1,16,320]{2,1,0:T(8,128)} async-done(((f32[16,16,320]{2,1,0:T(8,128)}), f32[1,16,320]{2,1,0:T(8,128)}) %reduce-scatter.2.cloned.1.call-update) | async-done | bytes 20496 | tf_op jit(solution)/shard_map/reduce_scatter | solution.py:57
  (257 shorter events, 54.4 us)
Async XLA Ops:
  8.1 9.1 %collective-permute-start = (f32[2,1,16,320]{3,2,1,0:T(8,128)S(1)}, f32[2,1,16,320]{3,2,1,0:T(8,128)S(1)}, u32[]{:S(2)}, u32[]{:S(2)}) collective-permute-start(f32[2,1,16,320]{3,2,1,0:T(8,128)S(1)} %slice.1129), channel_id=1, source_target_pairs={{16,0},{32,16},{48,32},{64,48},{80,64},{96,80},{112,96},{17,1},{33... | collective-permute-start | bytes 122888 | tf_op jit(solution)/shard_map/ppermute | solution.py:13
  10.9 15.1 %all-to-all-start = ((f32[16,1,16,320]{3,2,1,0:T(8,128)}), f32[16,1,16,320]{3,2,1,0:T(8,128)}, u32[]{:S(2)}, u32[]{:S(2)}) async-start(f32[16,1,16,320]{3,2,1,0:T(8,128)} %stack.331), calls=%async_computation | async-start | bytes 786432 | tf_op jit(solution)/shard_map/all_to_all | solution.py:63
  16.5 257.0 %reduce-scatter.2.cloned.1.call-start = ((), (), s32[]{:S(2)}) async-start(), calls=%async_computation.2 | async-start | bytes 417792 | tf_op jit(solution)/shard_map/reduce_scatter | solution.py:57
  18.9 6.3 %collective-permute-start.1 = (f32[2,1,16,320]{3,2,1,0:T(8,128)S(1)}, f32[2,1,16,320]{3,2,1,0:T(8,128)S(1)}, u32[]{:S(2)}, u32[]{:S(2)}) collective-permute-start(f32[2,1,16,320]{3,2,1,0:T(8,128)S(1)} %slice.1140), channel_id=1, source_target_pairs={{0,16},{16,32},{32,48},{48,64},{64,80},{80,96},{96,112},{1,17},{17... | collective-permute-start | bytes 122888 | tf_op jit(solution)/shard_map/ppermute | solution.py:13
  27.4 6.6 %collective-permute-start.2 = (f32[2,1,16,320]{3,2,1,0:T(8,128)S(1)}, f32[2,1,16,320]{3,2,1,0:T(8,128)S(1)}, u32[]{:S(2)}, u32[]{:S(2)}) collective-permute-start(f32[2,1,16,320]{3,2,1,0:T(8,128)S(1)} %slice.1153), channel_id=1, source_target_pairs={{16,0},{32,16},{48,32},{64,48},{80,64},{96,80},{112,96},{17,1},{33... | collective-permute-start | bytes 122888 | tf_op jit(solution)/shard_map/ppermute | solution.py:13
  35.6 5.7 %collective-permute-start.3 = (f32[2,1,16,320]{3,2,1,0:T(8,128)S(1)}, f32[2,1,16,320]{3,2,1,0:T(8,128)S(1)}, u32[]{:S(2)}, u32[]{:S(2)}) collective-permute-start(f32[2,1,16,320]{3,2,1,0:T(8,128)S(1)} %slice.1164), channel_id=1, source_target_pairs={{0,16},{16,32},{32,48},{48,64},{64,80},{80,96},{96,112},{1,17},{17... | collective-permute-start | bytes 122888 | tf_op jit(solution)/shard_map/ppermute | solution.py:13
  41.8 161.0 %copy-start.3 = (f32[16,16,320]{2,1,0:T(8,128)}, f32[16,16,320]{2,1,0:T(8,128)S(1)}, u32[]{:S(2)}) copy-start(f32[16,16,320]{2,1,0:T(8,128)S(1)} %get-tuple-element.158) | copy-start | bytes 983044
  41.8 161.0 %copy-start.5 = (f32[16,16,320]{2,1,0:T(8,128)}, f32[16,16,320]{2,1,0:T(8,128)S(1)}, u32[]{:S(2)}) copy-start(f32[16,16,320]{2,1,0:T(8,128)S(1)} %get-tuple-element.159) | copy-start | bytes 983044
  41.8 161.0 %copy-start.7 = (f32[16,16,320]{2,1,0:T(8,128)}, f32[16,16,320]{2,1,0:T(8,128)S(1)}, u32[]{:S(2)}) copy-start(f32[16,16,320]{2,1,0:T(8,128)S(1)} %get-tuple-element.160) | copy-start | bytes 983044
  42.2 8.7 %collective-permute-start.4 = (f32[2,1,16,320]{3,2,1,0:T(8,128)S(1)}, f32[2,1,16,320]{3,2,1,0:T(8,128)S(1)}, u32[]{:S(2)}, u32[]{:S(2)}) collective-permute-start(f32[2,1,16,320]{3,2,1,0:T(8,128)S(1)} %slice.1177), channel_id=1, source_target_pairs={{16,0},{32,16},{48,32},{64,48},{80,64},{96,80},{112,96},{17,1},{33... | collective-permute-start | bytes 122888 | tf_op jit(solution)/shard_map/ppermute | solution.py:13
  51.6 9.6 %collective-permute-start.5 = (f32[2,1,16,320]{3,2,1,0:T(8,128)S(1)}, f32[2,1,16,320]{3,2,1,0:T(8,128)S(1)}, u32[]{:S(2)}, u32[]{:S(2)}) collective-permute-start(f32[2,1,16,320]{3,2,1,0:T(8,128)S(1)} %slice.1188), channel_id=1, source_target_pairs={{0,16},{16,32},{32,48},{48,64},{64,80},{80,96},{96,112},{1,17},{17... | collective-permute-start | bytes 122888 | tf_op jit(solution)/shard_map/ppermute | solution.py:13
  61.7 141.1 %copy-start.16 = (f32[16,16,320]{2,1,0:T(8,128)}, f32[16,16,320]{2,1,0:T(8,128)S(1)}, u32[]{:S(2)}) copy-start(f32[16,16,320]{2,1,0:T(8,128)S(1)} %get-tuple-element.142) | copy-start | bytes 983044
  61.7 141.1 %copy-start.17 = (f32[16,16,320]{2,1,0:T(8,128)}, f32[16,16,320]{2,1,0:T(8,128)S(1)}, u32[]{:S(2)}) copy-start(f32[16,16,320]{2,1,0:T(8,128)S(1)} %get-tuple-element.143) | copy-start | bytes 983044
  61.8 141.1 %copy-start.18 = (f32[16,16,320]{2,1,0:T(8,128)}, f32[16,16,320]{2,1,0:T(8,128)S(1)}, u32[]{:S(2)}) copy-start(f32[16,16,320]{2,1,0:T(8,128)S(1)} %get-tuple-element.144) | copy-start | bytes 983044
  62.2 6.3 %collective-permute-start.6 = (f32[2,1,16,320]{3,2,1,0:T(8,128)S(1)}, f32[2,1,16,320]{3,2,1,0:T(8,128)S(1)}, u32[]{:S(2)}, u32[]{:S(2)}) collective-permute-start(f32[2,1,16,320]{3,2,1,0:T(8,128)S(1)} %slice.1201), channel_id=1, source_target_pairs={{16,0},{32,16},{48,32},{64,48},{80,64},{96,80},{112,96},{17,1},{33... | collective-permute-start | bytes 122888 | tf_op jit(solution)/shard_map/ppermute | solution.py:13
  69.3 9.3 %collective-permute-start.7 = (f32[2,1,16,320]{3,2,1,0:T(8,128)S(1)}, f32[2,1,16,320]{3,2,1,0:T(8,128)S(1)}, u32[]{:S(2)}, u32[]{:S(2)}) collective-permute-start(f32[2,1,16,320]{3,2,1,0:T(8,128)S(1)} %slice.1212), channel_id=1, source_target_pairs={{0,16},{16,32},{32,48},{48,64},{64,80},{80,96},{96,112},{1,17},{17... | collective-permute-start | bytes 122888 | tf_op jit(solution)/shard_map/ppermute | solution.py:13
  79.1 71.2 %copy-start.19 = (f32[16,16,320]{2,1,0:T(8,128)}, f32[16,16,320]{2,1,0:T(8,128)S(1)}, u32[]{:S(2)}) copy-start(f32[16,16,320]{2,1,0:T(8,128)S(1)} %get-tuple-element.126) | copy-start | bytes 983044
  79.1 71.2 %copy-start.20 = (f32[16,16,320]{2,1,0:T(8,128)}, f32[16,16,320]{2,1,0:T(8,128)S(1)}, u32[]{:S(2)}) copy-start(f32[16,16,320]{2,1,0:T(8,128)S(1)} %get-tuple-element.127) | copy-start | bytes 983044
  79.7 6.3 %collective-permute-start.8 = (f32[2,1,16,320]{3,2,1,0:T(8,128)S(1)}, f32[2,1,16,320]{3,2,1,0:T(8,128)S(1)}, u32[]{:S(2)}, u32[]{:S(2)}) collective-permute-start(f32[2,1,16,320]{3,2,1,0:T(8,128)S(1)} %slice.1225), channel_id=1, source_target_pairs={{16,0},{32,16},{48,32},{64,48},{80,64},{96,80},{112,96},{17,1},{33... | collective-permute-start | bytes 122888 | tf_op jit(solution)/shard_map/ppermute | solution.py:13
  86.9 9.3 %collective-permute-start.9 = (f32[2,1,16,320]{3,2,1,0:T(8,128)S(1)}, f32[2,1,16,320]{3,2,1,0:T(8,128)S(1)}, u32[]{:S(2)}, u32[]{:S(2)}) collective-permute-start(f32[2,1,16,320]{3,2,1,0:T(8,128)S(1)} %slice.1236), channel_id=1, source_target_pairs={{0,16},{16,32},{32,48},{48,64},{64,80},{80,96},{96,112},{1,17},{17... | collective-permute-start | bytes 122888 | tf_op jit(solution)/shard_map/ppermute | solution.py:13
  97.3 6.3 %collective-permute-start.10 = (f32[2,1,16,320]{3,2,1,0:T(8,128)S(1)}, f32[2,1,16,320]{3,2,1,0:T(8,128)S(1)}, u32[]{:S(2)}, u32[]{:S(2)}) collective-permute-start(f32[2,1,16,320]{3,2,1,0:T(8,128)S(1)} %slice.1249), channel_id=1, source_target_pairs={{16,0},{32,16},{48,32},{64,48},{80,64},{96,80},{112,96},{17,1},{33... | collective-permute-start | bytes 122888 | tf_op jit(solution)/shard_map/ppermute | solution.py:13
  104.6 9.3 %collective-permute-start.11 = (f32[2,1,16,320]{3,2,1,0:T(8,128)S(1)}, f32[2,1,16,320]{3,2,1,0:T(8,128)S(1)}, u32[]{:S(2)}, u32[]{:S(2)}) collective-permute-start(f32[2,1,16,320]{3,2,1,0:T(8,128)S(1)} %slice.1260), channel_id=1, source_target_pairs={{0,16},{16,32},{32,48},{48,64},{64,80},{80,96},{96,112},{1,17},{17... | collective-permute-start | bytes 122888 | tf_op jit(solution)/shard_map/ppermute | solution.py:13
  115.5 6.3 %collective-permute-start.12 = (f32[2,1,16,320]{3,2,1,0:T(8,128)S(1)}, f32[2,1,16,320]{3,2,1,0:T(8,128)S(1)}, u32[]{:S(2)}, u32[]{:S(2)}) collective-permute-start(f32[2,1,16,320]{3,2,1,0:T(8,128)S(1)} %slice.1273), channel_id=1, source_target_pairs={{16,0},{32,16},{48,32},{64,48},{80,64},{96,80},{112,96},{17,1},{33... | collective-permute-start | bytes 122888 | tf_op jit(solution)/shard_map/ppermute | solution.py:13
  123.4 9.3 %collective-permute-start.13 = (f32[2,1,16,320]{3,2,1,0:T(8,128)S(1)}, f32[2,1,16,320]{3,2,1,0:T(8,128)S(1)}, u32[]{:S(2)}, u32[]{:S(2)}) collective-permute-start(f32[2,1,16,320]{3,2,1,0:T(8,128)S(1)} %slice.1284), channel_id=1, source_target_pairs={{0,16},{16,32},{32,48},{48,64},{64,80},{80,96},{96,112},{1,17},{17... | collective-permute-start | bytes 122888 | tf_op jit(solution)/shard_map/ppermute | solution.py:13
  133.5 6.3 %collective-permute-start.14 = (f32[2,1,16,320]{3,2,1,0:T(8,128)S(1)}, f32[2,1,16,320]{3,2,1,0:T(8,128)S(1)}, u32[]{:S(2)}, u32[]{:S(2)}) collective-permute-start(f32[2,1,16,320]{3,2,1,0:T(8,128)S(1)} %slice.1297), channel_id=1, source_target_pairs={{16,0},{32,16},{48,32},{64,48},{80,64},{96,80},{112,96},{17,1},{33... | collective-permute-start | bytes 122888 | tf_op jit(solution)/shard_map/ppermute | solution.py:13
  140.5 9.3 %collective-permute-start.15 = (f32[2,1,16,320]{3,2,1,0:T(8,128)S(1)}, f32[2,1,16,320]{3,2,1,0:T(8,128)S(1)}, u32[]{:S(2)}, u32[]{:S(2)}) collective-permute-start(f32[2,1,16,320]{3,2,1,0:T(8,128)S(1)} %slice.1308), channel_id=1, source_target_pairs={{0,16},{16,32},{32,48},{48,64},{64,80},{80,96},{96,112},{1,17},{17... | collective-permute-start | bytes 122888 | tf_op jit(solution)/shard_map/ppermute | solution.py:13
  150.9 6.5 %collective-permute-start.16 = (f32[2,1,16,320]{3,2,1,0:T(8,128)S(1)}, f32[2,1,16,320]{3,2,1,0:T(8,128)S(1)}, u32[]{:S(2)}, u32[]{:S(2)}) collective-permute-start(f32[2,1,16,320]{3,2,1,0:T(8,128)S(1)} %slice.1321), channel_id=1, source_target_pairs={{16,0},{32,16},{48,32},{64,48},{80,64},{96,80},{112,96},{17,1},{33... | collective-permute-start | bytes 122888 | tf_op jit(solution)/shard_map/ppermute | solution.py:13
  158.1 9.7 %collective-permute-start.17 = (f32[2,1,16,320]{3,2,1,0:T(8,128)S(1)}, f32[2,1,16,320]{3,2,1,0:T(8,128)S(1)}, u32[]{:S(2)}, u32[]{:S(2)}) collective-permute-start(f32[2,1,16,320]{3,2,1,0:T(8,128)S(1)} %slice.1332), channel_id=1, source_target_pairs={{0,16},{16,32},{32,48},{48,64},{64,80},{80,96},{96,112},{1,17},{17... | collective-permute-start | bytes 122888 | tf_op jit(solution)/shard_map/ppermute | solution.py:13
  168.7 6.3 %collective-permute-start.18 = (f32[2,1,16,320]{3,2,1,0:T(8,128)S(1)}, f32[2,1,16,320]{3,2,1,0:T(8,128)S(1)}, u32[]{:S(2)}, u32[]{:S(2)}) collective-permute-start(f32[2,1,16,320]{3,2,1,0:T(8,128)S(1)} %slice.1345), channel_id=1, source_target_pairs={{16,0},{32,16},{48,32},{64,48},{80,64},{96,80},{112,96},{17,1},{33... | collective-permute-start | bytes 122888 | tf_op jit(solution)/shard_map/ppermute | solution.py:13
  175.8 9.3 %collective-permute-start.19 = (f32[2,1,16,320]{3,2,1,0:T(8,128)S(1)}, f32[2,1,16,320]{3,2,1,0:T(8,128)S(1)}, u32[]{:S(2)}, u32[]{:S(2)}) collective-permute-start(f32[2,1,16,320]{3,2,1,0:T(8,128)S(1)} %slice.1356), channel_id=1, source_target_pairs={{0,16},{16,32},{32,48},{48,64},{64,80},{80,96},{96,112},{1,17},{17... | collective-permute-start | bytes 122888 | tf_op jit(solution)/shard_map/ppermute | solution.py:13
  185.9 6.3 %collective-permute-start.20 = (f32[2,1,16,320]{3,2,1,0:T(8,128)S(1)}, f32[2,1,16,320]{3,2,1,0:T(8,128)S(1)}, u32[]{:S(2)}, u32[]{:S(2)}) collective-permute-start(f32[2,1,16,320]{3,2,1,0:T(8,128)S(1)} %slice.1369), channel_id=1, source_target_pairs={{16,0},{32,16},{48,32},{64,48},{80,64},{96,80},{112,96},{17,1},{33... | collective-permute-start | bytes 122888 | tf_op jit(solution)/shard_map/ppermute | solution.py:13
  193.1 9.3 %collective-permute-start.21 = (f32[2,1,16,320]{3,2,1,0:T(8,128)S(1)}, f32[2,1,16,320]{3,2,1,0:T(8,128)S(1)}, u32[]{:S(2)}, u32[]{:S(2)}) collective-permute-start(f32[2,1,16,320]{3,2,1,0:T(8,128)S(1)} %slice.1380), channel_id=1, source_target_pairs={{0,16},{16,32},{32,48},{48,64},{64,80},{80,96},{96,112},{1,17},{17... | collective-permute-start | bytes 122888 | tf_op jit(solution)/shard_map/ppermute | solution.py:13
  (21 other events, 329.2 us)
Sparse Core Ops, SparseCore 0:
  204.6 68.8 reduce-scatter.1
